TPU v7x, 256 devices: a whole 4x4x8 slice. The times are simulated.
256 devices in a mesh: rep: 32 (over z, y), tp: 8 (over x, core).
Axes of the slice: x: 4, y: 4, z: 8, core: 2. Of those that a mesh axis runs over, the one named last changes fastest.
Arguments:
- image_grads: bfloat16 [512, 48, 1280], P('rep', 'tp'), may hold values from -6 to 6
- dest_rank: int32 [512], P('rep'), may hold values from 0 to 31, as said below
- dest_slot: int32 [512], P('rep'), may hold values from 0 to 31, as said below
- saved_inputs: bfloat16 [1024, 48, 1280], P('rep'), may hold values from -6 to 6
- up_weight: bfloat16 [1280, 5120], P(None, 'tp'), may hold values from -0.15625 to 0.15625
- down_weight: bfloat16 [5120, 1280], P('tp'), may hold values from -0.078125 to 0.078125
- norm_gain: float32 [1280], replicated, may hold values from 0.25 to 1.75
Outputs:
- input_grads: bfloat16 [1024, 48, 1280], P('rep', 'tp')
- up_grads: float32 [1280, 5120], P('rep', 'tp')
- down_grads: float32 [5120, 1280], P('tp', 'rep')
- gain_grads: float32 [1280], replicated
Inputs may be any that keep to these rules, and one draw needn't show every extreme that they name: `dest_rank`: the images of one index of rep go to different owners; each owner receives at most 32 images, and some owner receives exactly 32 in every draw. `dest_slot`: the images that one owner receives have distinct slots 0, 1, ... up to their count less one; other slots hold no image.
All inputs are finite; a program needn't handle non-finite values.
Results may differ from a plain program's by a relative error of at most 0.015.
Values may be sent and summed in bfloat16 or wider, within the bound.
A program may use at most 128 MiB of HBM per device.

v0:
```python
import jax
import jax.numpy as jnp
from jax import lax
from jax.sharding import Mesh
from jax.sharding import PartitionSpec as P

REP = ("rep_0", "rep_1")
epsilon = 1e-05
gelu_c = 0.7978845608028654
gelu_a = 0.044715


def scatter_axes(value, axes, dim):
    if not axes:
        return value
    nearer = lax.psum_scatter(value, axes[0], scatter_dimension=dim, tiled=True)
    return scatter_axes(nearer, axes[1:], dim)


def sent_to_all(value, axis):
    copies = jnp.broadcast_to(value, (lax.axis_size(axis), *value.shape))
    return lax.all_to_all(copies, axis, split_axis=0, concat_axis=0, tiled=True)


def of_everyone(value, axis):
    everything = sent_to_all(value, axis)
    return jnp.sum(everything, axis=0)


def gelu_value(preact):
    inner = jnp.tanh(gelu_c * (preact + gelu_a * preact**3))
    return 0.5 * preact * (1.0 + inner)


def gelu_slope(preact):
    inner = jnp.tanh(gelu_c * (preact + gelu_a * preact**3))
    return 0.5 * (1.0 + inner) + 0.5 * preact * (1.0 - inner * inner) * gelu_c * (
        1.0 + 3.0 * gelu_a * preact * preact
    )


def outbound(images, dest_rank, dest_slot, groups, capacity):
    rank_ids = jnp.arange(groups, dtype=jnp.int32)
    one_hot = dest_rank[None, :] == rank_ids[:, None]
    packed = jnp.einsum(
        "ek,kpd->epd", one_hot.astype(jnp.bfloat16), images, preferred_element_type=jnp.float32
    ).astype(jnp.bfloat16)
    present = jnp.any(one_hot, axis=1)
    slot_sent = jnp.sum(jnp.where(one_hot, dest_slot[None, :], 0), axis=1) + jnp.where(
        present, 0, capacity
    )
    return (packed, slot_sent)


def compact(inbound, slot_recv, capacity):
    slot_ids = jnp.arange(capacity, dtype=jnp.int32)
    picker = (slot_recv[None, :] == slot_ids[:, None]).astype(jnp.bfloat16)
    return jnp.einsum("ce,epd->cpd", picker, inbound, preferred_element_type=jnp.float32).astype(
        jnp.bfloat16
    )


def local(image_grads, dest_rank, dest_slot, saved_inputs, up_weight, down_weight, norm_gain):
    groups = lax.axis_size(REP)
    capacity = saved_inputs.shape[0]
    patches = saved_inputs.shape[1]
    width = saved_inputs.shape[2]
    slab = image_grads.shape[1]
    packed, slot_sent = outbound(image_grads, dest_rank, dest_slot, groups, capacity)
    inbound, slot_recv = (
        lax.all_to_all(packed, REP, split_axis=0, concat_axis=0, tiled=True),
        lax.all_to_all(slot_sent, REP, split_axis=0, concat_axis=0, tiled=True),
    )
    routed = lax.all_gather(compact(inbound, slot_recv, capacity), "tp", axis=1, tiled=True)
    rows = capacity * patches
    grads = routed.reshape(rows, width)
    values = saved_inputs.reshape(rows, width).astype(jnp.float32)
    mean_v = jnp.mean(values, axis=1, keepdims=True)
    var_v = jnp.mean((values - mean_v) ** 2, axis=1, keepdims=True)
    inv_std = 1.0 / jnp.sqrt(var_v + epsilon)
    centred = (values - mean_v) * inv_std
    normed = (centred * norm_gain[None, :]).astype(jnp.bfloat16)
    preact = jnp.dot(normed, up_weight, preferred_element_type=jnp.float32)
    hidden = gelu_value(preact).astype(jnp.bfloat16)
    grad_hidden = jnp.dot(grads, down_weight.T, preferred_element_type=jnp.float32)
    grad_pre = (grad_hidden * gelu_slope(preact)).astype(jnp.bfloat16)
    down_local = jnp.dot(hidden.T, grads, preferred_element_type=jnp.float32)
    up_local = jnp.dot(normed.T, grad_pre, preferred_element_type=jnp.float32)
    partial_normed = jnp.dot(grad_pre, up_weight.T, preferred_element_type=jnp.float32)
    up_grads, down_grads = (
        scatter_axes(up_local.astype(jnp.bfloat16), REP, 0).astype(jnp.float32),
        scatter_axes(down_local.astype(jnp.bfloat16), REP, 1).astype(jnp.float32),
    )
    start = lax.axis_index("tp") * slab
    grad_normed = lax.psum(partial_normed.astype(jnp.bfloat16), "tp").astype(jnp.float32)
    gain_grads = of_everyone(jnp.sum(grad_normed * centred, axis=0), REP)
    scaled = grad_normed * norm_gain[None, :]
    first = jnp.mean(scaled, axis=1, keepdims=True)
    second = jnp.mean(scaled * centred, axis=1, keepdims=True)
    result = grads.astype(jnp.float32) + inv_std * (scaled - first - centred * second)
    result = result.reshape(capacity, patches, width)
    input_grads = lax.dynamic_slice_in_dim(result, start, slab, 1).astype(jnp.bfloat16)
    return (input_grads, up_grads, down_grads, gain_grads)


def solution(mesh):
    split = Mesh(mesh.devices.reshape(8, 4, mesh.shape["tp"]), ("rep_0", "rep_1", "tp"))
    return jax.shard_map(
        local,
        mesh=split,
        in_specs=(
            P(REP, "tp", None),
            P(REP),
            P(REP),
            P(REP, None, None),
            P(None, "tp"),
            P("tp", None),
            P(),
        ),
        out_specs=(P(REP, "tp", None), P(REP, "tp"), P("tp", REP), P()),
        check_vma=False,
    )
```

profile of v0, /device:TPU:2, one launch (start us, length us, event | category | flops | bytes accessed | tf_op | source)
XLA Modules:
  0.0 318.9 jit_solution(2042661000471552826)
XLA Ops:
  7.2 0.9 fusion.27
  8.0 0.8 select_reduce_fusion
  8.8 0.7 copy.29
  9.5 11.5 %all-to-all-start = ((s32[32,1,1]{2,1,0:T(1,128)}), s32[32,1,1]{2,1,0:T(1,128)S(1)}, u32[]{:S(2)}, u32[]{:S(2)}) async-start(s32[32,1,1]{2,1,0:T(1,128)} %copy.29), calls=%async_computation | async-start | bytes 32768 | tf_op jit(solution)/shard_map/all_to_all | solution.py:72
  21.0 1.4 convolution_convert_fusion.4
  22.4 1.1 copy.30
  23.5 7.2 %all-to-all-done = s32[32,1,1]{2,1,0:T(1,128)S(1)} async-done(((s32[32,1,1]{2,1,0:T(1,128)}), s32[32,1,1]{2,1,0:T(1,128)S(1)}, u32[]{:S(2)}, u32[]{:S(2)}) %all-to-all-start) | async-done | bytes 160 | tf_op jit(solution)/shard_map/all_to_all | solution.py:72
  30.7 3.9 %all-to-all-start.1 = ((bf16[32,6,1280]{2,1,0:T(8,128)(2,1)}), bf16[32,6,1280]{2,1,0:T(8,128)(2,1)S(1)}, u32[]{:S(2)}, u32[]{:S(2)}) async-start(bf16[32,6,1280]{2,1,0:T(8,128)(2,1)} %copy.30), calls=%async_computation.1 | async-start | bytes 1310720 | tf_op jit(solution)/shard_map/all_to_all | solution.py:71
  34.6 0.0 all-gather.2.cloned.1.call-start
  34.6 0.7 reduce.3
  35.3 18.5 %all-to-all-done.1 = bf16[32,6,1280]{2,1,0:T(8,128)(2,1)S(1)} async-done(((bf16[32,6,1280]{2,1,0:T(8,128)(2,1)}), bf16[32,6,1280]{2,1,0:T(8,128)(2,1)S(1)}, u32[]{:S(2)}, u32[]{:S(2)}) %all-to-all-start.1) | async-done | bytes 491552 | tf_op jit(solution)/shard_map/all_to_all | solution.py:71
  53.8 1.1 convolution_convert_fusion.3
  54.8 0.0 all-gather.2.cloned.1.call-update
  54.9 0.2 reduce-scatter.11.cloned.1.call-start
  55.1 2.7 convert_reduce_fusion
  57.8 0.1 div.18
  57.9 3.3 %multiply_reduce_fusion = f32[32,48]{1,0:T(8,128)S(1)} fusion(bf16[32,48,1280]{2,1,0:T(8,128)(2,1)} %param.10, f32[32,48]{1,0:T(8,128)S(1)} %broadcast_multiply_fusion), kind=kLoop, calls=%fused_computation.13 | loop fusion | flops 7862784 | bytes 3944448 | tf_op jit(solution)/shard_map/reduce_sum | solution.py:79
  61.2 0.1 sqrt.6
  61.3 3.0 multiply_convert_fusion
  64.3 2.0 copy-done.2
  66.3 5.2 %fusion.34 = f32[1536,640]{1,0:T(8,128)} fusion(bf16[1536,1280]{1,0:T(8,128)(2,1)S(1)} %multiply_convert_fusion, bf16[1280,640]{1,0:T(8,128)(2,1)S(1)} %copy-done), kind=kOutput, calls=%fused_computation.56 | convolution fusion | flops 2516582400 | bytes 9502720 | tf_op jit(solution)/shard_map/dot_general | solution.py:83
  71.5 12.3 %all-gather.2.cloned.1.call-done = bf16[32,48,1280]{2,0,1:T(8,128)(2,1)} async-done(((bf16[32,6,1280]{2,0,1:T(8,128)(2,1)}), bf16[32,48,1280]{2,0,1:T(8,128)(2,1)}) %all-gather.2.cloned.1.call-update) | async-done | bytes 3932176 | tf_op jit(solution)/shard_map/all_gather | solution.py:74
  83.8 4.4 %copy.32 = bf16[32,48,1280]{2,1,0:T(8,128)(2,1)S(1)} copy(bf16[32,48,1280]{2,0,1:T(8,128)(2,1)} %all-gather.2.cloned.1.call-done) | data formatting | bytes 7864320 | tf_op jit(solution)/shard_map/all_gather | solution.py:74
  88.2 1.9 copy-done.1
  90.1 5.1 %convolution_convert_fusion.1 = bf16[640,1280]{0,1:T(8,128)(2,1)} fusion(bf16[1536,1280]{1,0:T(8,128)(2,1)S(1)} %bitcast.34, f32[1536,640]{1,0:T(8,128)S(1)} %copy-done.5), kind=kOutput, calls=%fused_computation.28 | convolution fusion | flops 2526248960 | bytes 9502720 | tf_op jit(solution)/shard_map/dot_general | solution.py:87
  95.2 0.3 all-reduce.4.cloned.1.call-start
  95.5 8.2 %fusion.17 = bf16[1536,640]{1,0:T(8,128)(2,1)S(1)} fusion(f32[1536,640]{1,0:T(8,128)} %fusion.34, bf16[1536,1280]{1,0:T(8,128)(2,1)} %bitcast.35, bf16[640,1280]{1,0:T(8,128)(2,1)S(1)} %copy-done.4), kind=kOutput, calls=%fused_computation.26 | convolution fusion | flops 2535260160 | bytes 11468800 | tf_op jit(solution)/shard_map/dot_general | solution.py:85
  103.7 1.3 copy-done.6
  104.9 4.7 %convolution_convert_fusion = bf16[1536,1280]{1,0:T(8,128)(2,1)} fusion(bf16[1536,640]{1,0:T(8,128)(2,1)S(1)} %fusion.17, bf16[1280,640]{1,0:T(8,128)(2,1)S(1)} %copy-done), kind=kOutput, calls=%fused_computation.14 | convolution fusion | flops 2518548480 | bytes 7536640 | tf_op jit(solution)/shard_map/dot_general | solution.py:89
  109.7 0.0 all-reduce.4.cloned.1.call-update
  109.7 0.0 reduce-scatter.9.cloned.1.call-start
  109.7 7.2 %convolution_convert_fusion.2 = bf16[1280,640]{1,0:T(8,128)(2,1)} fusion(bf16[1536,1280]{1,0:T(8,128)(2,1)} %copy-done.2, bf16[1536,640]{1,0:T(8,128)(2,1)} %copy-done.6), kind=kOutput, calls=%fused_computation.29 | convolution fusion | flops 2517401600 | bytes 7536640 | tf_op jit(solution)/shard_map/dot_general | solution.py:88
  116.9 0.0 reduce-scatter.15.cloned.1.call-start
  117.0 20.4 %reduce-scatter.11.cloned.1.call-done = bf16[640,160]{0,1:T(8,128)(2,1)} async-done(((bf16[640,1280]{0,1:T(8,128)(2,1)}), bf16[640,160]{0,1:T(8,128)(2,1)}) %reduce-scatter.11.cloned.1.call-update) | async-done | bytes 204816 | tf_op jit(solution)/shard_map/reduce_scatter | solution.py:16
  137.4 74.8 %all-reduce.4.cloned.1.call-done = bf16[1536,1280]{1,0:T(8,128)(2,1)} async-done(((bf16[1536,1280]{1,0:T(8,128)(2,1)}), bf16[1536,1280]{1,0:T(8,128)(2,1)}) %all-reduce.4.cloned.1.call-update) | async-done | bytes 3932176 | tf_op jit(solution)/shard_map/psum | solution.py:95
  212.2 5.8 %fusion.7 = (f32[1280]{0:T(1024)S(1)}, f32[1536]{0:T(1024)S(1)}, f32[1536]{0:T(1024)S(1)}) fusion(bf16[1536,1280]{1,0:T(8,128)(2,1)} %all-reduce.4.cloned.1.call-done, bf16[32,48,1280]{2,1,0:T(8,128)(2,1)} %param.10, f32[1536]{0:T(1024)S(1)} %div.18, f32[1536]{0:T(1024)S(1)} %sqrt.6, f32[1280]{0:T(1024)S(1)} %copy-done.3), kind=kLoop, calls=%fused_computation.9 | loop fusion | flops 19656448 | bytes 7899136 | tf_op jit(solution)/shard_map/reduce_sum | solution.py:96
  218.0 0.7 broadcast_in_dim.38
  218.8 9.9 %all-to-all-start.2 = ((f32[32,1,1280]{2,1,0:T(1,128)}), f32[32,1,1280]{2,1,0:T(1,128)S(1)}, u32[]{:S(2)}, u32[]{:S(2)}) async-start(f32[32,1,1280]{2,1,0:T(1,128)} %broadcast_in_dim.38), calls=%async_computation.4 | async-start | bytes 327680 | tf_op jit(solution)/shard_map/all_to_all | solution.py:22
  228.6 0.0 reduce-scatter.13.cloned.1.call-start
  228.7 31.9 %reduce-scatter.9.cloned.1.call-done = bf16[160,640]{1,0:T(8,128)(2,1)} async-done(((bf16[1280,640]{1,0:T(8,128)(2,1)}), bf16[160,640]{1,0:T(8,128)(2,1)}) %reduce-scatter.9.cloned.1.call-update) | async-done | bytes 204816 | tf_op jit(solution)/shard_map/reduce_scatter | solution.py:16
  260.6 6.1 %fusion.5 = bf16[1536,1280]{1,0:T(8,128)(2,1)S(1)} fusion(bf16[1536,1280]{1,0:T(8,128)(2,1)} %all-reduce.4.cloned.1.call-done, bf16[32,48,1280]{2,1,0:T(8,128)(2,1)} %param.10, f32[1536]{0:T(1024)S(1)} %get-tuple-element.7, f32[1536]{0:T(1024)S(1)} %get-tuple-element.8, f32[1280]{0:T(1024)S(1)} %copy-done.3, f32[1536]{0:T(1024)S(1)} %div.18, ...), kind=kLoop, calls=%fused_computation.7 | loop fusion | flops 23592960 | bytes 15758336 | tf_op jit(solution)/shard_map/add | solution.py:100
  266.7 0.2 constant_dynamic-slice_fusion
  266.9 0.9 copy.40
  267.8 0.7 reduce_sum.69
  268.5 16.8 %reduce-scatter.15.cloned.1.call-done = bf16[640,40]{0,1:T(8,128)(2,1)} async-done(((bf16[640,160]{0,1:T(8,128)(2,1)}), bf16[640,40]{0,1:T(8,128)(2,1)}) %reduce-scatter.15.cloned.1.call-update) | async-done | bytes 51216
  285.3 1.5 convert_element_type.66
  286.8 23.8 %reduce-scatter.13.cloned.1.call-done = bf16[40,640]{1,0:T(8,128)(2,1)} async-done(((bf16[160,640]{1,0:T(8,128)(2,1)}), bf16[40,640]{1,0:T(8,128)(2,1)}) %reduce-scatter.13.cloned.1.call-update) | async-done | bytes 51216
  310.6 1.5 convert_element_type.63
  (20 shorter events, 0.1 us)
Async XLA Ops:
  7.2 59.1 %copy-start = (bf16[1280,640]{1,0:T(8,128)(2,1)S(1)}, bf16[1280,640]{1,0:T(8,128)(2,1)}, u32[]{:S(2)}) copy-start(bf16[1280,640]{1,0:T(8,128)(2,1)} %param.11) | copy-start | bytes 4915204
  9.5 21.2 %all-to-all-start = ((s32[32,1,1]{2,1,0:T(1,128)}), s32[32,1,1]{2,1,0:T(1,128)S(1)}, u32[]{:S(2)}, u32[]{:S(2)}) async-start(s32[32,1,1]{2,1,0:T(1,128)} %copy.29), calls=%async_computation | async-start | bytes 32768 | tf_op jit(solution)/shard_map/all_to_all | solution.py:72
  30.7 23.1 %all-to-all-start.1 = ((bf16[32,6,1280]{2,1,0:T(8,128)(2,1)}), bf16[32,6,1280]{2,1,0:T(8,128)(2,1)S(1)}, u32[]{:S(2)}, u32[]{:S(2)}) async-start(bf16[32,6,1280]{2,1,0:T(8,128)(2,1)} %copy.30), calls=%async_computation.1 | async-start | bytes 1310720 | tf_op jit(solution)/shard_map/all_to_all | solution.py:71
  34.6 49.2 %all-gather.2.cloned.1.call-start = ((), (), s32[]{:S(2)}) async-start(), calls=%async_computation.7 | async-start | bytes 4423680 | tf_op jit(solution)/shard_map/all_gather | solution.py:74
  54.8 6.4 %copy-start.3 = (f32[1280]{0:T(1024)S(1)}, f32[1280]{0:T(1024)}, u32[]{:S(2)}) copy-start(f32[1280]{0:T(1024)} %param.13) | copy-start | bytes 15364
  54.9 82.5 %reduce-scatter.11.cloned.1.call-start = ((), (), s32[]{:S(2)}) async-start(), calls=%async_computation.10 | async-start | bytes 1843200 | tf_op jit(solution)/shard_map/reduce_scatter | solution.py:16
  64.3 2.0 copy-start.2
  83.8 6.3 %copy-start.5 = (f32[1536,640]{1,0:T(8,128)S(1)}, f32[1536,640]{1,0:T(8,128)}, u32[]{:S(2)}) copy-start(f32[1536,640]{1,0:T(8,128)} %fusion.34) | copy-start | bytes 11796484
  88.2 1.9 copy-start.1
  90.1 5.4 %copy-start.4 = (bf16[640,1280]{1,0:T(8,128)(2,1)S(1)}, bf16[640,1280]{1,0:T(8,128)(2,1)}, u32[]{:S(2)}) copy-start(bf16[640,1280]{1,0:T(8,128)(2,1)} %param.12) | copy-start | bytes 4915204
  95.2 117.0 %all-reduce.4.cloned.1.call-start = ((), (), s32[]{:S(2)}) async-start(), calls=%async_computation.8 | async-start | bytes 7864320 | tf_op jit(solution)/shard_map/psum | solution.py:95
  103.7 1.3 copy-start.6
  109.7 150.9 %reduce-scatter.9.cloned.1.call-start = ((), (), s32[]{:S(2)}) async-start(), calls=%async_computation.9 | async-start | bytes 1843200 | tf_op jit(solution)/shard_map/reduce_scatter | solution.py:16
  116.9 168.4 %reduce-scatter.15.cloned.1.call-start = ((), (), s32[]{:S(2)}) async-start(), calls=%async_computation.12 | async-start | bytes 256000
  218.8 49.0 %all-to-all-start.2 = ((f32[32,1,1280]{2,1,0:T(1,128)}), f32[32,1,1280]{2,1,0:T(1,128)S(1)}, u32[]{:S(2)}, u32[]{:S(2)}) async-start(f32[32,1,1280]{2,1,0:T(1,128)} %broadcast_in_dim.38), calls=%async_computation.4 | async-start | bytes 327680 | tf_op jit(solution)/shard_map/all_to_all | solution.py:22
  228.6 82.0 %reduce-scatter.13.cloned.1.call-start = ((), (), s32[]{:S(2)}) async-start(), calls=%async_computation.11 | async-start | bytes 256000
Sparse Core Ops, SparseCore 0:
  55.0 28.8 all-gather.1
  95.3 41.9 reduce-scatter.10
  139.7 72.4 all-reduce.3
  214.6 45.9 reduce-scatter.8
  263.0 22.2 reduce-scatter.14
  287.7 22.8 reduce-scatter.12
where the time goes:
time: 319 us
  waiting for transfers between devices  206 us (65%)
  matrix products  32.8 us (10%)
  other arithmetic  26.8 us (8%)
  starting transfers between devices  25.9 us (8%)
  between operations  14.3 us (4%)
  local copies, waits for them, and re-layouts  13.3 us (4%)
    psum x1, waiting for transfers between devices, local(): lax.psum(partial_normed.astype(jnp.bfloat16), 'tp').astype(jnp.float32)  74.8 us
    reduce_scatter x2, waiting for transfers between devices, scatter_axes(): nearer = lax.psum_scatter(value, axes[0], scatter_dimension=dim, tiled=True)  52.3 us
    unnamed x8, waiting for transfers between devices  40.7 us
    all_to_all x1, waiting for transfers between devices, local(): lax.all_to_all(packed, REP, split_axis=0, concat_axis=0, tiled=True)  18.5 us
    all_gather x1, waiting for transfers between devices, local(): lax.all_gather(compact(inbound, slot_recv, capacity), 'tp', axis=1, tiled...  12.3 us
    all_to_all x1, starting transfers between devices, local(): lax.all_to_all(slot_sent, REP, split_axis=0, concat_axis=0, tiled=True)  11.5 us
    all_to_all x1, starting transfers between devices, sent_to_all(): return lax.all_to_all(copies, axis, split_axis=0, concat_axis=0, tiled=True)  9.85 us
    dot_general x1, matrix products, local(): jnp.dot(grads, down_weight.T, preferred_element_type=jnp.float32)  8.16 us
  transfers between devices with their start and end apart: 9, of which 8 were waited for; matrix products, arithmetic and copies ran while one was open for 17% of the time, Pallas kernels for 0%

commit v1 on v0

--- a/solution.py
+++ b/solution.py
@@ -71,7 +71,22 @@
         lax.all_to_all(packed, REP, split_axis=0, concat_axis=0, tiled=True),
         lax.all_to_all(slot_sent, REP, split_axis=0, concat_axis=0, tiled=True),
     )
-    routed = lax.all_gather(compact(inbound, slot_recv, capacity), "tp", axis=1, tiled=True)
+    value_2 = compact(inbound, slot_recv, capacity)
+    ways, here, step = (lax.axis_size("tp"), lax.axis_index("tp"), value_2.shape[1])
+    lengths = [n * ways if d == 1 else n for d, n in enumerate(value_2.shape)]
+    full = lax.dynamic_update_slice_in_dim(
+        jnp.zeros(lengths, value_2.dtype), value_2, here * step, axis=1
+    )
+    going_up = going_down = value_2
+    for far in range(1, ways // 2 + 1):
+        going_up = lax.ppermute(going_up, "tp", [(d, (d + 1) % ways) for d in range(ways)])
+        full = lax.dynamic_update_slice_in_dim(full, going_up, (here - far) % ways * step, axis=1)
+        if 2 * far < ways:
+            going_down = lax.ppermute(going_down, "tp", [(d, (d - 1) % ways) for d in range(ways)])
+            full = lax.dynamic_update_slice_in_dim(
+                full, going_down, (here + far) % ways * step, axis=1
+            )
+    routed = full
     rows = capacity * patches
     grads = routed.reshape(rows, width)
     values = saved_inputs.reshape(rows, width).astype(jnp.float32)

time: 319 us -> 304 us (0.953)
  waiting for transfers between devices: 206 us -> 121 us
  local copies, waits for them, and re-layouts: 13.3 us -> 69.6 us
  starting transfers between devices: 25.9 us -> 30.4 us
  matrix products: 32.8 us -> 37 us
    dynamic_update_slice x0 -> x8, local copies, waits for them, and re-layouts: none -> 54.9 us  [the longest x4 27.1 us: local(): lax.dynamic_update_slice_in_dim(full, going_up, (here - far) % ways * ste...]
    reduce_scatter x2, waiting for transfers between devices: 52.3 us -> 19.2 us  [scatter_axes(): nearer = lax.psum_scatter(value, axes[0], scatter_dimension=dim, tiled=True)]
    psum x1, waiting for transfers between devices: 74.8 us -> 48.2 us  [local(): lax.psum(partial_normed.astype(jnp.bfloat16), 'tp').astype(jnp.float32)]
    unnamed x8 -> x7, waiting for transfers between devices: 40.7 us -> 15.8 us
    all_gather x1 -> x0, waiting for transfers between devices: 12.3 us -> none  [local(): lax.all_gather(compact(inbound, slot_recv, capacity), 'tp', axis=1, tiled...]
    ppermute x0 -> x7, waiting for transfers between devices: none -> 9.47 us  [the longest x4 9.46 us: local(): lax.ppermute(going_up, 'tp', [(d, (d + 1) % ways) for d in range(ways)])]
    ppermute x0 -> x7, local copies, waits for them, and re-layouts: none -> 7.1 us  [the longest x3 3.93 us: local(): lax.ppermute(going_down, 'tp', [(d, (d - 1) % ways) for d in range(ways)])]
    ppermute x0 -> x7, starting transfers between devices: none -> 4.89 us  [the longest x3 4.87 us: local(): lax.ppermute(going_down, 'tp', [(d, (d - 1) % ways) for d in range(ways)])]
  transfers between devices with their start and end apart: 9 -> 15, of which waited for: 8 -> 9; matrix products, arithmetic and copies ran while one was open for 17% -> 37% of each run, Pallas kernels for 0% -> 0%
where the time goes in v1:
time: 304 us; the launch traced here: 302 us
  waiting for transfers between devices  121 us (40%)
  local copies, waits for them, and re-layouts  69.6 us (23%)
  matrix products  37 us (12%)
  starting transfers between devices  30.4 us (10%)
  other arithmetic  28.4 us (9%)
  between operations  15.4 us (5%)
    psum x1, waiting for transfers between devices, local(): lax.psum(partial_normed.astype(jnp.bfloat16), 'tp').astype(jnp.float32)  48.2 us
    dynamic_update_slice x4, local copies, waits for them, and re-layouts, local(): lax.dynamic_update_slice_in_dim(full, going_up, (here - far) % ways * ste...  27.1 us
    dynamic_update_slice x3, local copies, waits for them, and re-layouts, local(): lax.dynamic_update_slice_in_dim(full, going_down, (here + far) % ways * s...  20.8 us
    reduce_scatter x2, waiting for transfers between devices, scatter_axes(): nearer = lax.psum_scatter(value, axes[0], scatter_dimension=dim, tiled=True)  19.2 us
    all_to_all x1, waiting for transfers between devices, local(): lax.all_to_all(packed, REP, split_axis=0, concat_axis=0, tiled=True)  18.5 us
    unnamed x7, waiting for transfers between devices  15.8 us
    all_to_all x1, starting transfers between devices, local(): lax.all_to_all(slot_sent, REP, split_axis=0, concat_axis=0, tiled=True)  11.5 us
    all_to_all x1, starting transfers between devices, sent_to_all(): return lax.all_to_all(copies, axis, split_axis=0, concat_axis=0, tiled=True)  9.7 us
  transfers between devices with their start and end apart: 15, of which 9 were waited for; matrix products, arithmetic and copies ran while one was open for 37% of the time, Pallas kernels for 0%

profile of v1, /device:TPU:2, one launch (start us, length us, event | category | flops | bytes accessed | tf_op | source)
XLA Modules:
  0.0 302.1 jit_solution(9688536662383769436)
XLA Ops:
  8.0 0.9 fusion.27
  8.9 0.8 select_reduce_fusion
  10.3 11.5 %all-to-all-start = ((s32[32,1,1]{2,1,0:T(1,128)}), s32[32,1,1]{2,1,0:T(1,128)S(1)}, u32[]{:S(2)}, u32[]{:S(2)}) async-start(s32[32,1,1]{2,1,0:T(1,128)} %copy.55), calls=%async_computation | async-start | bytes 32768 | tf_op jit(solution)/shard_map/all_to_all | solution.py:72
  21.8 1.4 convolution_convert_fusion.4
  23.2 1.1 copy.56
  24.3 7.2 %all-to-all-done = s32[32,1,1]{2,1,0:T(1,128)S(1)} async-done(((s32[32,1,1]{2,1,0:T(1,128)}), s32[32,1,1]{2,1,0:T(1,128)S(1)}, u32[]{:S(2)}, u32[]{:S(2)}) %all-to-all-start) | async-done | bytes 160 | tf_op jit(solution)/shard_map/all_to_all | solution.py:72
  31.5 3.9 %all-to-all-start.1 = ((bf16[32,6,1280]{2,1,0:T(8,128)(2,1)}), bf16[32,6,1280]{2,1,0:T(8,128)(2,1)S(1)}, u32[]{:S(2)}, u32[]{:S(2)}) async-start(bf16[32,6,1280]{2,1,0:T(8,128)(2,1)} %copy.56), calls=%async_computation.1 | async-start | bytes 1310720 | tf_op jit(solution)/shard_map/all_to_all | solution.py:71
  36.1 18.5 %all-to-all-done.1 = bf16[32,6,1280]{2,1,0:T(8,128)(2,1)S(1)} async-done(((bf16[32,6,1280]{2,1,0:T(8,128)(2,1)}), bf16[32,6,1280]{2,1,0:T(8,128)(2,1)S(1)}, u32[]{:S(2)}, u32[]{:S(2)}) %all-to-all-start.1) | async-done | bytes 491552 | tf_op jit(solution)/shard_map/all_to_all | solution.py:71
  54.9 2.7 convert_reduce_fusion
  57.7 1.7 collective-permute-start.1
  59.4 3.7 %collective-permute-done = bf16[32,6,1280]{2,0,1:T(8,128)(2,1)S(1)} collective-permute-done((bf16[32,6,1280]{2,0,1:T(8,128)(2,1)S(1)}, bf16[32,6,1280]{2,0,1:T(8,128)(2,1)S(1)}, u32[]{:S(2)}, u32[]{:S(2)}) %collective-permute-start) | collective-permute-done | bytes 491552 | tf_op jit(solution)/shard_map/ppermute | solution.py:82
  63.2 3.5 %multiply_reduce_fusion = f32[32,48]{1,0:T(8,128)S(1)} fusion(bf16[32,48,1280]{2,1,0:T(8,128)(2,1)} %param.10, f32[32,48]{1,0:T(8,128)S(1)} %broadcast_multiply_fusion), kind=kLoop, calls=%fused_computation.13 | loop fusion | flops 7862784 | bytes 3944448 | tf_op jit(solution)/shard_map/reduce_sum | solution.py:94
  66.7 1.6 collective-permute-start.3
  68.3 3.2 %collective-permute-done.2 = bf16[32,6,1280]{2,0,1:T(8,128)(2,1)} collective-permute-done((bf16[32,6,1280]{2,0,1:T(8,128)(2,1)S(1)}, bf16[32,6,1280]{2,0,1:T(8,128)(2,1)}, u32[]{:S(2)}, u32[]{:S(2)}) %collective-permute-start.2) | collective-permute-done | bytes 491552 | tf_op jit(solution)/shard_map/ppermute | solution.py:82
  71.5 4.4 %multiply_convert_fusion = bf16[1536,1280]{1,0:T(8,128)(2,1)} fusion(bf16[32,48,1280]{2,1,0:T(8,128)(2,1)} %param.10, f32[1280]{0:T(1024)S(1)} %copy-done.3, f32[1536]{0:T(1024)S(1)} %div.18, f32[1536]{0:T(1024)S(1)} %sqrt.6), kind=kLoop, calls=%fused_computation.12 | loop fusion | flops 9830400 | bytes 7881728 | tf_op jit(solution)/shard_map/convert_element_type | solution.py:97
  75.9 1.6 collective-permute-start.5
  77.5 2.5 collective-permute-done.4
  80.0 7.2 %fusion.34 = f32[1536,640]{1,0:T(8,128)} fusion(bf16[1536,1280]{1,0:T(8,128)(2,1)} %multiply_convert_fusion, bf16[1280,640]{1,0:T(8,128)(2,1)S(1)} %copy-done), kind=kOutput, calls=%fused_computation.56 | convolution fusion | flops 2516582400 | bytes 9502720 | tf_op jit(solution)/shard_map/dot_general | solution.py:98
  87.5 2.2 broadcast_in_dim.24
  89.7 7.0 %dynamic_update_slice.24 = bf16[32,48,1280]{2,1,0:T(8,128)(2,1)} dynamic-update-slice(bf16[32,48,1280]{2,1,0:T(8,128)(2,1)} %broadcast_in_dim.24, bf16[32,6,1280]{2,1,0:T(8,128)(2,1)S(1)} %copy.58, s32[]{:T(128)} %constant.65.clone.1, s32[]{:T(128)S(6)} %select_n.74, s32[]{:T(128)} %constant.65.clone.1) | dynamic-update-slice | bytes 983044 | tf_op jit(solution)/shard_map/dynamic_update_slice | solution.py:77
  97.0 6.9 %dynamic_update_slice.25 = bf16[32,48,1280]{2,1,0:T(8,128)(2,1)} dynamic-update-slice(bf16[32,48,1280]{2,1,0:T(8,128)(2,1)} %dynamic_update_slice.24, bf16[32,6,1280]{2,1,0:T(8,128)(2,1)S(1)} %copy.59, s32[]{:T(128)} %constant.65.clone.1, s32[]{:T(128)S(6)} %select_n.76, s32[]{:T(128)} %constant.65.clone.1) | dynamic-update-slice | bytes 983044 | tf_op jit(solution)/shard_map/dynamic_update_slice | solution.py:83
  103.9 1.3 copy.60
  105.2 7.0 %dynamic_update_slice.26 = bf16[32,48,1280]{2,1,0:T(8,128)(2,1)} dynamic-update-slice(bf16[32,48,1280]{2,1,0:T(8,128)(2,1)} %dynamic_update_slice.25, bf16[32,6,1280]{2,1,0:T(8,128)(2,1)S(1)} %copy.60, s32[]{:T(128)} %constant.65.clone.1, s32[]{:T(128)S(6)} %select_n.78, s32[]{:T(128)} %constant.65.clone.1) | dynamic-update-slice | bytes 983044 | tf_op jit(solution)/shard_map/dynamic_update_slice | solution.py:86
  112.2 1.3 copy.61
  113.5 6.9 %dynamic_update_slice.27 = bf16[32,48,1280]{2,1,0:T(8,128)(2,1)} dynamic-update-slice(bf16[32,48,1280]{2,1,0:T(8,128)(2,1)} %dynamic_update_slice.26, bf16[32,6,1280]{2,1,0:T(8,128)(2,1)S(1)} %copy.61, s32[]{:T(128)} %constant.65.clone.1, s32[]{:T(128)S(6)} %select_n.80, s32[]{:T(128)} %constant.65.clone.1) | dynamic-update-slice | bytes 983044 | tf_op jit(solution)/shard_map/dynamic_update_slice | solution.py:83
  120.5 1.3 copy.62
  121.8 6.9 %dynamic_update_slice.28 = bf16[32,48,1280]{2,1,0:T(8,128)(2,1)} dynamic-update-slice(bf16[32,48,1280]{2,1,0:T(8,128)(2,1)} %dynamic_update_slice.27, bf16[32,6,1280]{2,1,0:T(8,128)(2,1)S(1)} %copy.62, s32[]{:T(128)} %constant.65.clone.1, s32[]{:T(128)S(6)} %select_n.82, s32[]{:T(128)} %constant.65.clone.1) | dynamic-update-slice | bytes 983044 | tf_op jit(solution)/shard_map/dynamic_update_slice | solution.py:86
  129.0 6.3 %dynamic_update_slice.29 = bf16[32,48,1280]{2,1,0:T(8,128)(2,1)} dynamic-update-slice(bf16[32,48,1280]{2,1,0:T(8,128)(2,1)} %dynamic_update_slice.28, bf16[32,6,1280]{2,1,0:T(8,128)(2,1)S(1)} %copy.63, s32[]{:T(128)} %constant.65.clone.1, s32[]{:T(128)S(6)} %select_n.84, s32[]{:T(128)} %constant.65.clone.1) | dynamic-update-slice | bytes 983044 | tf_op jit(solution)/shard_map/dynamic_update_slice | solution.py:83
  135.3 1.3 copy.64
  136.6 6.9 %dynamic_update_slice.30 = bf16[32,48,1280]{2,1,0:T(8,128)(2,1)} dynamic-update-slice(bf16[32,48,1280]{2,1,0:T(8,128)(2,1)} %dynamic_update_slice.29, bf16[32,6,1280]{2,1,0:T(8,128)(2,1)S(1)} %copy.64, s32[]{:T(128)} %constant.65.clone.1, s32[]{:T(128)S(6)} %select_n.86, s32[]{:T(128)} %constant.65.clone.1) | dynamic-update-slice | bytes 983044 | tf_op jit(solution)/shard_map/dynamic_update_slice | solution.py:86
  143.5 1.3 copy.65
  144.8 6.9 %dynamic_update_slice.31 = bf16[32,48,1280]{2,1,0:T(8,128)(2,1)} dynamic-update-slice(bf16[32,48,1280]{2,1,0:T(8,128)(2,1)} %dynamic_update_slice.30, bf16[32,6,1280]{2,1,0:T(8,128)(2,1)S(1)} %copy.65, s32[]{:T(128)} %constant.65.clone.1, s32[]{:T(128)S(6)} %select_n.88, s32[]{:T(128)} %constant.65.clone.1) | dynamic-update-slice | bytes 983044 | tf_op jit(solution)/shard_map/dynamic_update_slice | solution.py:83
  151.8 8.0 %convolution_convert_fusion.1 = bf16[640,1280]{0,1:T(8,128)(2,1)} fusion(bf16[1536,1280]{1,0:T(8,128)(2,1)} %bitcast.34, f32[1536,640]{1,0:T(8,128)} %fusion.34), kind=kOutput, calls=%fused_computation.28 | convolution fusion | flops 2526248960 | bytes 9502720 | tf_op jit(solution)/shard_map/dot_general | solution.py:102
  160.1 8.2 %fusion.17 = bf16[1536,640]{1,0:T(8,128)(2,1)S(1)} fusion(f32[1536,640]{1,0:T(8,128)} %fusion.34, bf16[1536,1280]{1,0:T(8,128)(2,1)} %bitcast.35, bf16[640,1280]{1,0:T(8,128)(2,1)S(1)} %copy-done.4), kind=kOutput, calls=%fused_computation.26 | convolution fusion | flops 2535260160 | bytes 11468800 | tf_op jit(solution)/shard_map/dot_general | solution.py:100
  168.3 1.3 copy-done.5
  169.6 4.8 %convolution_convert_fusion = bf16[1536,1280]{1,0:T(8,128)(2,1)} fusion(bf16[1536,640]{1,0:T(8,128)(2,1)S(1)} %fusion.17, bf16[1280,640]{1,0:T(8,128)(2,1)S(1)} %copy-done), kind=kOutput, calls=%fused_computation.14 | convolution fusion | flops 2518548480 | bytes 7536640 | tf_op jit(solution)/shard_map/dot_general | solution.py:104
  174.4 7.2 %convolution_convert_fusion.2 = bf16[1280,640]{1,0:T(8,128)(2,1)} fusion(bf16[1536,1280]{1,0:T(8,128)(2,1)} %multiply_convert_fusion, bf16[1536,640]{1,0:T(8,128)(2,1)} %copy-done.5), kind=kOutput, calls=%fused_computation.29 | convolution fusion | flops 2517401600 | bytes 7536640 | tf_op jit(solution)/shard_map/dot_general | solution.py:103
  181.6 19.2 %reduce-scatter.11.cloned.1.call-done = bf16[640,160]{0,1:T(8,128)(2,1)} async-done(((bf16[640,1280]{0,1:T(8,128)(2,1)}), bf16[640,160]{0,1:T(8,128)(2,1)}) %reduce-scatter.11.cloned.1.call-update) | async-done | bytes 204816 | tf_op jit(solution)/shard_map/reduce_scatter | solution.py:16
  200.8 48.2 %all-reduce.4.cloned.1.call-done = bf16[1536,1280]{1,0:T(8,128)(2,1)} async-done(((bf16[1536,1280]{1,0:T(8,128)(2,1)}), bf16[1536,1280]{1,0:T(8,128)(2,1)}) %all-reduce.4.cloned.1.call-update) | async-done | bytes 3932176 | tf_op jit(solution)/shard_map/psum | solution.py:110
  249.0 5.8 %fusion.7 = (f32[1280]{0:T(1024)S(1)}, f32[1536]{0:T(1024)S(1)}, f32[1536]{0:T(1024)S(1)}) fusion(bf16[1536,1280]{1,0:T(8,128)(2,1)} %all-reduce.4.cloned.1.call-done, bf16[32,48,1280]{2,1,0:T(8,128)(2,1)} %param.10, f32[1536]{0:T(1024)S(1)} %div.18, f32[1536]{0:T(1024)S(1)} %sqrt.6, f32[1280]{0:T(1024)S(1)} %copy-done.3), kind=kLoop, calls=%fused_computation.9 | loop fusion | flops 19656448 | bytes 7899136 | tf_op jit(solution)/shard_map/reduce_sum | solution.py:111
  254.8 0.7 broadcast_in_dim.42
  255.6 9.7 %all-to-all-start.2 = ((f32[32,1,1280]{2,1,0:T(1,128)}), f32[32,1,1280]{2,1,0:T(1,128)S(1)}, u32[]{:S(2)}, u32[]{:S(2)}) async-start(f32[32,1,1280]{2,1,0:T(1,128)} %broadcast_in_dim.42), calls=%async_computation.4 | async-start | bytes 327680 | tf_op jit(solution)/shard_map/all_to_all | solution.py:22
  265.9 6.1 %fusion.5 = bf16[1536,1280]{1,0:T(8,128)(2,1)S(1)} fusion(bf16[1536,1280]{1,0:T(8,128)(2,1)} %all-reduce.4.cloned.1.call-done, bf16[32,48,1280]{2,1,0:T(8,128)(2,1)} %param.10, f32[1536]{0:T(1024)S(1)} %get-tuple-element.7, f32[1536]{0:T(1024)S(1)} %get-tuple-element.8, f32[1280]{0:T(1024)S(1)} %copy-done.3, f32[1536]{0:T(1024)S(1)} %div.18, ...), kind=kLoop, calls=%fused_computation.7 | loop fusion | flops 23592960 | bytes 15758336 | tf_op jit(solution)/shard_map/add | solution.py:115
  272.2 0.9 copy.73
  273.0 3.0 %all-to-all-done.2 = f32[32,1,1280]{2,1,0:T(1,128)S(1)} async-done(((f32[32,1,1280]{2,1,0:T(1,128)}), f32[32,1,1280]{2,1,0:T(1,128)S(1)}, u32[]{:S(2)}, u32[]{:S(2)}) %all-to-all-start.2) | async-done | bytes 163872 | tf_op jit(solution)/shard_map/all_to_all | solution.py:22
  276.8 1.5 convert_element_type.66
  278.3 15.3 %reduce-scatter.13.cloned.1.call-done = bf16[40,640]{1,0:T(8,128)(2,1)} async-done(((bf16[160,640]{1,0:T(8,128)(2,1)}), bf16[40,640]{1,0:T(8,128)(2,1)}) %reduce-scatter.13.cloned.1.call-update) | async-done | bytes 51216
  293.5 1.5 convert_element_type.63
  (45 shorter events, 4.6 us)
Async XLA Ops:
  8.0 72.0 %copy-start = (bf16[1280,640]{1,0:T(8,128)(2,1)S(1)}, bf16[1280,640]{1,0:T(8,128)(2,1)}, u32[]{:S(2)}) copy-start(bf16[1280,640]{1,0:T(8,128)(2,1)} %param.11) | copy-start | bytes 4915204
  10.3 21.2 %all-to-all-start = ((s32[32,1,1]{2,1,0:T(1,128)}), s32[32,1,1]{2,1,0:T(1,128)S(1)}, u32[]{:S(2)}, u32[]{:S(2)}) async-start(s32[32,1,1]{2,1,0:T(1,128)} %copy.55), calls=%async_computation | async-start | bytes 32768 | tf_op jit(solution)/shard_map/all_to_all | solution.py:72
  31.5 23.1 %all-to-all-start.1 = ((bf16[32,6,1280]{2,1,0:T(8,128)(2,1)}), bf16[32,6,1280]{2,1,0:T(8,128)(2,1)S(1)}, u32[]{:S(2)}, u32[]{:S(2)}) async-start(bf16[32,6,1280]{2,1,0:T(8,128)(2,1)} %copy.56), calls=%async_computation.1 | async-start | bytes 1310720 | tf_op jit(solution)/shard_map/all_to_all | solution.py:71
  35.4 165.4 %reduce-scatter.11.cloned.1.call-start = ((), (), s32[]{:S(2)}) async-start(), calls=%async_computation.9 | async-start | bytes 1843200 | tf_op jit(solution)/shard_map/reduce_scatter | solution.py:16
  54.9 16.6 %copy-start.3 = (f32[1280]{0:T(1024)S(1)}, f32[1280]{0:T(1024)}, u32[]{:S(2)}) copy-start(f32[1280]{0:T(1024)} %param.13) | copy-start | bytes 15364
  54.9 8.3 %collective-permute-start = (bf16[32,6,1280]{2,0,1:T(8,128)(2,1)S(1)}, bf16[32,6,1280]{2,0,1:T(8,128)(2,1)S(1)}, u32[]{:S(2)}, u32[]{:S(2)}) collective-permute-start(bf16[32,6,1280]{2,0,1:T(8,128)(2,1)S(1)} %convolution_convert_fusion.3), channel_id=1, source_target_pairs={{0,1},{1,2},{2,3},{3,4},{4,5},{5,6},{6,7},{7,0},{8,9},{9,10},{10,1... | collective-permute-start | bytes 1474568 | tf_op jit(solution)/shard_map/ppermute | solution.py:82
  57.7 9.0 %collective-permute-start.1 = (bf16[32,6,1280]{2,0,1:T(8,128)(2,1)S(1)}, bf16[32,6,1280]{2,0,1:T(8,128)(2,1)}, u32[]{:S(2)}, u32[]{:S(2)}) collective-permute-start(bf16[32,6,1280]{2,0,1:T(8,128)(2,1)S(1)} %convolution_convert_fusion.3), channel_id=1, source_target_pairs={{0,7},{1,0},{2,1},{3,2},{4,3},{5,4},{6,5},{7,6},{8,15},{9,8},{10,9... | collective-permute-start | bytes 1474568 | tf_op jit(solution)/shard_map/ppermute | solution.py:85
  63.2 12.7 %copy-start.1 = (bf16[32,6,1280]{2,0,1:T(8,128)(2,1)}, bf16[32,6,1280]{2,0,1:T(8,128)(2,1)S(1)}, u32[]{:S(2)}) copy-start(bf16[32,6,1280]{2,0,1:T(8,128)(2,1)S(1)} %collective-permute-done) | copy-start | bytes 1474564
  63.2 8.4 %collective-permute-start.2 = (bf16[32,6,1280]{2,0,1:T(8,128)(2,1)S(1)}, bf16[32,6,1280]{2,0,1:T(8,128)(2,1)}, u32[]{:S(2)}, u32[]{:S(2)}) collective-permute-start(bf16[32,6,1280]{2,0,1:T(8,128)(2,1)S(1)} %collective-permute-done), channel_id=1, source_target_pairs={{0,1},{1,2},{2,3},{3,4},{4,5},{5,6},{6,7},{7,0},{8,9},{9,10},{10,1... | collective-permute-start | bytes 1474568 | tf_op jit(solution)/shard_map/ppermute | solution.py:82
  66.7 9.2 %collective-permute-start.3 = (bf16[32,6,1280]{2,0,1:T(8,128)(2,1)}, bf16[32,6,1280]{2,0,1:T(8,128)(2,1)}, u32[]{:S(2)}, u32[]{:S(2)}) collective-permute-start(bf16[32,6,1280]{2,0,1:T(8,128)(2,1)} %collective-permute-done.1), channel_id=1, source_target_pairs={{0,7},{1,0},{2,1},{3,2},{4,3},{5,4},{6,5},{7,6},{8,15},{9,8},{10,9... | collective-permute-start | bytes 1474568 | tf_op jit(solution)/shard_map/ppermute | solution.py:85
  71.5 8.5 %collective-permute-start.4 = (bf16[32,6,1280]{2,0,1:T(8,128)(2,1)}, bf16[32,6,1280]{2,0,1:T(8,128)(2,1)S(1)}, u32[]{:S(2)}, u32[]{:S(2)}) collective-permute-start(bf16[32,6,1280]{2,0,1:T(8,128)(2,1)} %collective-permute-done.2), channel_id=1, source_target_pairs={{0,1},{1,2},{2,3},{3,4},{4,5},{5,6},{6,7},{7,0},{8,9},{9,10},{10,1... | collective-permute-start | bytes 1474568 | tf_op jit(solution)/shard_map/ppermute | solution.py:82
  75.9 59.4 %collective-permute-start.5 = (bf16[32,6,1280]{2,0,1:T(8,128)(2,1)}, bf16[32,6,1280]{2,0,1:T(8,128)(2,1)}, u32[]{:S(2)}, u32[]{:S(2)}) collective-permute-start(bf16[32,6,1280]{2,0,1:T(8,128)(2,1)} %collective-permute-done.3), channel_id=1, source_target_pairs={{0,7},{1,0},{2,1},{3,2},{4,3},{5,4},{6,5},{7,6},{8,15},{9,8},{10,9... | collective-permute-start | bytes 1474568 | tf_op jit(solution)/shard_map/ppermute | solution.py:85
  80.0 63.5 %collective-permute-start.6 = (bf16[32,6,1280]{2,0,1:T(8,128)(2,1)S(1)}, bf16[32,6,1280]{2,0,1:T(8,128)(2,1)}, u32[]{:S(2)}, u32[]{:S(2)}) collective-permute-start(bf16[32,6,1280]{2,0,1:T(8,128)(2,1)S(1)} %collective-permute-done.4), channel_id=1, source_target_pairs={{0,1},{1,2},{2,3},{3,4},{4,5},{5,6},{6,7},{7,0},{8,9},{9,10},{10,1... | collective-permute-start | bytes 1474568 | tf_op jit(solution)/shard_map/ppermute | solution.py:82
  87.5 9.2 %copy-start.2 = (bf16[32,6,1280]{2,0,1:T(8,128)(2,1)S(1)}, bf16[32,6,1280]{2,0,1:T(8,128)(2,1)}, u32[]{:S(2)}) copy-start(bf16[32,6,1280]{2,0,1:T(8,128)(2,1)} %copy-done.1) | copy-start | bytes 1474564
  151.8 8.3 %copy-start.4 = (bf16[640,1280]{1,0:T(8,128)(2,1)S(1)}, bf16[640,1280]{1,0:T(8,128)(2,1)}, u32[]{:S(2)}) copy-start(bf16[640,1280]{1,0:T(8,128)(2,1)} %param.12) | copy-start | bytes 4915204
  159.8 89.2 %all-reduce.4.cloned.1.call-start = ((), (), s32[]{:S(2)}) async-start(), calls=%async_computation.7 | async-start | bytes 7864320 | tf_op jit(solution)/shard_map/psum | solution.py:110
  168.3 1.3 copy-start.5
  174.3 91.0 %reduce-scatter.9.cloned.1.call-start = ((), (), s32[]{:S(2)}) async-start(), calls=%async_computation.8 | async-start | bytes 1843200 | tf_op jit(solution)/shard_map/reduce_scatter | solution.py:16
  181.6 95.2 %reduce-scatter.15.cloned.1.call-start = ((), (), s32[]{:S(2)}) async-start(), calls=%async_computation.11 | async-start | bytes 256000
  255.6 20.5 %all-to-all-start.2 = ((f32[32,1,1280]{2,1,0:T(1,128)}), f32[32,1,1280]{2,1,0:T(1,128)S(1)}, u32[]{:S(2)}, u32[]{:S(2)}) async-start(f32[32,1,1280]{2,1,0:T(1,128)} %broadcast_in_dim.42), calls=%async_computation.4 | async-start | bytes 327680 | tf_op jit(solution)/shard_map/all_to_all | solution.py:22
  265.3 28.2 %reduce-scatter.13.cloned.1.call-start = ((), (), s32[]{:S(2)}) async-start(), calls=%async_computation.10 | async-start | bytes 256000
Sparse Core Ops, SparseCore 0:
  160.0 40.8 reduce-scatter.10
  203.4 39.5 reduce-scatter.8
  245.5 21.5 reduce-scatter.14
  269.5 23.9 reduce-scatter.12
Sparse Core Ops, SparseCore 1:
  174.4 74.5 all-reduce.3
